TPU v7x, 256 devices: a whole 4x4x8 slice. The times are simulated.
256 devices in a mesh: replica: 16 (over z, core), tile: 16 (over x, y).
Axes of the slice: x: 4, y: 4, z: 8, core: 2. Of those that a mesh axis runs over, the one named last changes fastest.
Arguments:
- public_tokens: bfloat16 [4096, 5120], P('replica', 'tile'), may hold values from -6 to 6
- public_targets: bfloat16 [4096, 4096], P(('replica', 'tile')), may hold values from -6 to 6
- private_tokens: bfloat16 [6144, 5120], P('replica', 'tile'), may hold values from -6 to 6
- private_targets: bfloat16 [6144, 4096], P(('replica', 'tile')), may hold values from -6 to 6
- token_counts: int32 [16, 3], P('replica'), may hold values from 1 to 128, 320 in all within a row
- weight: float32 [5120, 4096], P('tile', 'replica'), may hold values from -0.078125 to 0.078125
- public_moment: float32 [5120, 4096], P('tile', 'replica'), may hold values from 1 to 10
- adam_first: float32 [5120, 4096], P('tile', 'replica'), may hold values from -3 to 3
- adam_second: float32 [5120, 4096], P('tile', 'replica'), may hold values from 0.1 to 1
- noise_draw: float32 [5120, 4096], P('tile', 'replica'), may hold values from -6 to 6
Outputs:
- new_weight: float32 [5120, 4096], P('tile', 'replica')
- new_first: float32 [5120, 4096], P('tile', 'replica')
- new_second: float32 [5120, 4096], P('tile', 'replica')
- new_public: float32 [5120, 4096], P('tile', 'replica')
Inputs may be any that keep to these rules, and one draw needn't show every extreme that they name: `token_counts`: each row holds the live token counts of one replica's 3 private examples; every row sums to 320 and its largest entry is 128.
All inputs are finite; a program needn't handle non-finite values.
Results may differ from a plain program's by a relative error of at most 0.0031.
Values may be sent and summed in bfloat16 or wider, within the bound.
No kernel may reach another device: no remote copies, remote signals or barrier semaphores. Data moves between devices by JAX's collectives and lax.ppermute only.
A program may use at most 64 MiB of HBM per device.

v0:
```python
import math
import jax
import jax.numpy as jnp
from jax import lax
from jax.sharding import PartitionSpec as P

D = 5120
L = 128
Q = 4096
beta_first = 0.9
beta_second = 0.99
beta_public = 0.9
public_epsilon = 0.001
adam_epsilon = 1e-08
clip_factor = 0.6
noise_level = 4.0
learn_rate = 0.01
contract_rows = (((0,), (0,)), ((), ()))


def slot_owner(first_row, span, seq_len):
    rows_at = first_row + jnp.arange(span, dtype=jnp.int32)
    return (rows_at, rows_at // seq_len)


def per_slot(owners, values):
    picks = jnp.arange(values.shape[0], dtype=jnp.int32)
    return jnp.sum(jnp.where(owners[:, None] == picks[None, :], values[None, :], 0), axis=1)


def live_slots(first_row, span, counts_row, seq_len):
    rows_at, owners = slot_owner(first_row, span, seq_len)
    return rows_at % seq_len < per_slot(owners, counts_row)


def on_device(
    public_tokens,
    public_targets,
    private_tokens,
    private_targets,
    token_counts,
    weight,
    public_moment,
    adam_first,
    adam_second,
    noise_draw,
):
    replicas = lax.axis_size("replica")
    tile_pos = lax.axis_index("tile")
    seq_len = L
    w_half = lax.all_gather(weight.astype(jnp.bfloat16), "replica", axis=1, tiled=True)
    public_total = public_tokens.shape[0] * replicas
    block_x = public_tokens
    public_out = lax.psum_scatter(
        jnp.dot(block_x, w_half, preferred_element_type=jnp.float32),
        "tile",
        scatter_dimension=0,
        tiled=True,
    )
    public_delta = (public_out - public_targets.astype(jnp.float32)).astype(jnp.bfloat16)
    block_x = public_tokens
    public_grad = lax.dot_general(
        block_x,
        lax.all_gather(public_delta, "tile", axis=0, tiled=True),
        contract_rows,
        preferred_element_type=jnp.float32,
    )
    grad_owned = lax.psum_scatter(
        public_grad, "replica", scatter_dimension=1, tiled=True
    ) / math.sqrt(public_total)
    new_public = beta_public * public_moment + (1.0 - beta_public) * grad_owned * grad_owned
    precond_owned = 1.0 / (jnp.sqrt(new_public) + public_epsilon)
    precond = lax.all_gather(precond_owned, "replica", axis=1, tiled=True)
    counts_row = token_counts[0]
    slots_all = private_tokens.shape[0]
    slot_rows = private_targets.shape[0]
    block_x = private_tokens
    private_out = lax.psum_scatter(
        jnp.dot(block_x, w_half, preferred_element_type=jnp.float32),
        "tile",
        scatter_dimension=0,
        tiled=True,
    )
    local_live = live_slots(tile_pos * slot_rows, slot_rows, counts_row, seq_len)
    local_delta = jnp.where(
        local_live[:, None], private_out - private_targets.astype(jnp.float32), 0.0
    ).astype(jnp.bfloat16)
    private_delta = lax.all_gather(local_delta, "tile", axis=0, tiled=True)

    def example_norm(example):
        first_row = example * seq_len
        block_x = lax.dynamic_slice_in_dim(private_tokens, first_row, seq_len, 0)
        block_d = lax.dynamic_slice_in_dim(private_delta, first_row, seq_len, 0)
        grads = lax.dot_general(block_x, block_d, contract_rows, preferred_element_type=jnp.float32)
        scaled = grads * precond
        return jnp.sum(scaled * scaled)

    examples_here = token_counts.shape[1]
    partial_norms = lax.map(example_norm, jnp.arange(examples_here, dtype=jnp.int32))
    squares = lax.psum(partial_norms, "tile")
    clip_norm = clip_factor * math.sqrt(L * D * Q)
    factors = clip_norm / jnp.maximum(jnp.sqrt(squares), clip_norm)
    rows_at, owners = slot_owner(0, slots_all, seq_len)
    slot_factor = per_slot(owners, factors)
    weighted = (slot_factor[:, None] * private_delta.astype(jnp.float32)).astype(jnp.bfloat16)
    summed = precond * lax.dot_general(
        private_tokens, weighted, contract_rows, preferred_element_type=jnp.float32
    )
    summed_owned = lax.psum_scatter(summed, "replica", scatter_dimension=1, tiled=True)
    examples_total = examples_here * replicas
    noise_scale = noise_level * clip_factor * math.sqrt(L)
    gradient = (summed_owned + noise_scale * noise_draw) / examples_total
    new_first = beta_first * adam_first + (1.0 - beta_first) * gradient
    new_second = beta_second * adam_second + (1.0 - beta_second) * gradient * gradient
    first_hat = new_first / (1.0 - beta_first**2)
    second_hat = new_second / (1.0 - beta_second**2)
    new_weight = weight - learn_rate * first_hat / (jnp.sqrt(second_hat) + adam_epsilon)
    return (new_weight, new_first, new_second, new_public)


def solution(mesh):
    placed = (
        P("replica", "tile"),
        P(("replica", "tile"), None),
        P("replica", "tile"),
        P(("replica", "tile"), None),
        P("replica", None),
        P("tile", "replica"),
        P("tile", "replica"),
        P("tile", "replica"),
        P("tile", "replica"),
        P("tile", "replica"),
    )
    return jax.shard_map(
        on_device,
        mesh=mesh,
        in_specs=placed,
        out_specs=(
            P("tile", "replica"),
            P("tile", "replica"),
            P("tile", "replica"),
            P("tile", "replica"),
        ),
        check_vma=False,
    )
```

profile of v0, /device:TPU:2, one launch (start us, length us, event | category | flops | bytes accessed | tf_op | source)
XLA Modules:
  0.0 588.4 jit_solution(9840578557947384932)
XLA Ops:
  7.2 0.0 copy-start
  7.2 0.0 all-gather.5.cloned.1.call-start
  7.2 1.7 convert_element_type.23
  8.9 0.0 all-gather.5.cloned.1.call-update
  8.9 0.0 copy-start.9
  9.0 0.0 copy-start.2
  9.0 0.0 reduce-scatter.7.cloned.1.call-start
  9.0 46.8 %all-gather.5.cloned.1.call-done = bf16[320,4096]{1,0:T(8,128)(2,1)} async-done(((bf16[320,256]{1,0:T(8,128)(2,1)}), bf16[320,4096]{1,0:T(8,128)(2,1)}) %all-gather.5.cloned.1.call-update) | async-done | bytes 2621456 | tf_op jit(solution)/shard_map/all_gather | solution.py:51
  55.8 0.0 copy-done
  55.8 0.0 copy-start.1
  55.8 5.2 fusion.11
  61.0 0.0 reduce-scatter.7.cloned.1.call-update
  61.1 0.0 all-gather.7.cloned.1.call-start
  61.1 82.5 %reduce-scatter.7.cloned.1.call-done = f32[16,4096]{1,0:T(8,128)} async-done(((f32[256,4096]{1,0:T(8,128)}), f32[16,4096]{1,0:T(8,128)}) %reduce-scatter.7.cloned.1.call-update) | async-done | bytes 262160 | tf_op jit(solution)/shard_map/reduce_scatter | solution.py:54
  143.6 0.0 copy-done.9
  143.6 1.6 subtract_convert_fusion
  145.2 0.0 all-gather.7.cloned.1.call-update
  145.2 0.0 reduce-scatter.13.cloned.1.call-start
  145.3 0.0 copy-done.2
  145.3 0.0 copy-done.1
  145.3 4.5 fusion.12
  149.8 0.0 reduce-scatter.13.cloned.1.call-update
  149.9 0.0 reduce-scatter.9.cloned.1.call-start
  149.9 45.9 %all-gather.7.cloned.1.call-done = bf16[256,4096]{1,0:T(8,128)(2,1)} async-done(((bf16[16,4096]{1,0:T(8,128)(2,1)}), bf16[256,4096]{1,0:T(8,128)(2,1)}) %all-gather.7.cloned.1.call-update) | async-done | bytes 2097168 | tf_op jit(solution)/shard_map/all_gather | solution.py:64
  195.8 4.8 convolution_bitcast_fusion.1
  200.6 0.0 copy-start.10
  200.6 0.0 copy-start.8
  200.6 0.0 copy-start.4
  200.6 0.0 reduce-scatter.9.cloned.1.call-update
  200.6 0.0 all-gather.11.cloned.1.call-start
  200.7 0.6 copy-done.10
  201.3 0.1 select_reduce_fusion.1
  201.4 84.1 %reduce-scatter.13.cloned.1.call-done = f32[24,4096]{1,0:T(8,128)} async-done(((f32[384,4096]{1,0:T(8,128)}), f32[24,4096]{1,0:T(8,128)}) %reduce-scatter.13.cloned.1.call-update) | async-done | bytes 393232
  285.5 0.0 copy-done.8
  285.5 1.8 select_convert_fusion
  287.3 0.0 all-gather.11.cloned.1.call-update
  287.3 0.0 all-gather.9.cloned.1.call-start
  287.3 65.5 %reduce-scatter.9.cloned.1.call-done = f32[320,256]{1,0:T(8,128)} async-done(((f32[320,4096]{1,0:T(8,128)}), f32[320,256]{1,0:T(8,128)}) %reduce-scatter.9.cloned.1.call-update) | async-done | bytes 327696 | tf_op jit(solution)/shard_map/reduce_scatter | solution.py:68
  352.8 0.0 copy-done.4
  352.8 1.9 add_divide_fusion
  354.8 0.0 all-gather.9.cloned.1.call-update
  354.8 0.0 reduce-scatter.11.cloned.1.call-start
  354.8 51.4 %all-gather.11.cloned.1.call-done = bf16[384,4096]{1,0:T(8,128)(2,1)} async-done(((bf16[24,4096]{1,0:T(8,128)(2,1)}), bf16[384,4096]{1,0:T(8,128)(2,1)}) %all-gather.11.cloned.1.call-update) | async-done | bytes 3145744 | tf_op jit(solution)/shard_map/all_gather | solution.py:88
  406.3 45.5 %all-gather.9.cloned.1.call-done = f32[320,4096]{1,0:T(8,128)} async-done(((f32[320,256]{1,0:T(8,128)}), f32[320,4096]{1,0:T(8,128)}) %all-gather.9.cloned.1.call-update) | async-done | bytes 5242896 | tf_op jit(solution)/shard_map/all_gather | solution.py:73
  451.7 20.8 %while.10 = (s32[]{:T(128)}, f32[3]{0:T(128)S(1)}, s32[3]{0:T(128)S(1)}, bf16[384,320]{0,1:T(8,128)(2,1)S(1)}, bf16[384,4096]{1,0:T(8,128)(2,1)}, /*index=5*/f32...) while((s32[]{:T(128)}, f32[3]{0:T(128)S(1)}, s32[3]{0:T(128)S(1)}, ...), condition=%wide.region_6.7_spmd, body=%wide.region_4.6_spmd.sunk | while | flops 339476480 | bytes 6374575 | solution.py:99
  451.7 0.6 dynamic_slice.19
  453.0 4.9 fusion.25
  457.9 0.8 dynamic_update_slice.5
  458.7 0.6 dynamic_slice.19
  459.9 5.0 fusion.25
  464.9 0.8 dynamic_update_slice.5
  465.6 0.6 dynamic_slice.19
  466.9 5.0 fusion.25
  471.8 0.8 dynamic_update_slice.5
  472.6 34.3 %psum.7 = f32[3]{0:T(128)S(1)} all-reduce(f32[3]{0:T(128)S(1)} %get-tuple-element.36), channel_id=1, replica_groups=mesh['replica'=16,'tile'=16] {'tile'}, use_global_device_ids=true, to_apply=%region_7.8 | all-reduce | flops 3 | bytes 24 | tf_op jit(solution)/shard_map/psum | solution.py:100
  506.8 0.1 select_reduce_fusion
  506.9 7.4 %fusion.5 = f32[320,4096]{1,0:T(8,128)} fusion(f32[320,4096]{1,0:T(8,128)} %get-tuple-element.130, bf16[384,320]{0,1:T(8,128)(2,1)S(1)} %get-tuple-element.142, bf16[384,4096]{1,0:T(8,128)(2,1)} %get-tuple-element.138, f32[384]{0:T(512)S(1)} %select_reduce_fusion), kind=kOutput, calls=%fused_computation.9 | convolution fusion | flops 1012662272 | bytes 13878784 | tf_op jit(solution)/shard_map/dot_general | solution.py:106
  514.4 0.0 reduce-scatter.11.cloned.1.call-update
  514.4 65.1 %reduce-scatter.11.cloned.1.call-done = f32[320,256]{1,0:T(8,128)} async-done(((f32[320,4096]{1,0:T(8,128)}), f32[320,256]{1,0:T(8,128)}) %reduce-scatter.11.cloned.1.call-update) | async-done | bytes 327696 | tf_op jit(solution)/shard_map/reduce_scatter | solution.py:109
  579.5 0.0 copy-done.3
  579.5 0.0 copy-done.5
  579.5 0.0 copy-done.6
  579.5 0.0 copy-done.7
  579.5 2.1 divide_subtract_fusion
  (10 shorter events, 0.1 us)
Async XLA Ops:
  7.2 48.6 %copy-start = (bf16[256,320]{0,1:T(8,128)(2,1)S(1)}, bf16[256,320]{0,1:T(8,128)(2,1)}, u32[]{:S(2)}) copy-start(bf16[256,320]{0,1:T(8,128)(2,1)} %param.12) | copy-start | bytes 491524
  7.2 48.6 %all-gather.5.cloned.1.call-start = ((), (), s32[]{:S(2)}) async-start(), calls=%async_computation.4 | async-start | bytes 2785280 | tf_op jit(solution)/shard_map/all_gather | solution.py:51
  8.9 134.6 %copy-start.9 = (bf16[16,4096]{1,0:T(8,128)(2,1)S(1)}, bf16[16,4096]{1,0:T(8,128)(2,1)}, u32[]{:S(2)}) copy-start(bf16[16,4096]{1,0:T(8,128)(2,1)} %param.13) | copy-start | bytes 393220
  9.0 136.3 %copy-start.2 = (bf16[384,320]{0,1:T(8,128)(2,1)S(1)}, bf16[384,320]{0,1:T(8,128)(2,1)}, u32[]{:S(2)}) copy-start(bf16[384,320]{0,1:T(8,128)(2,1)} %param.14) | copy-start | bytes 737284
  9.0 134.6 %reduce-scatter.7.cloned.1.call-start = ((), (), s32[]{:S(2)}) async-start(), calls=%async_computation.5 | async-start | bytes 4456448 | tf_op jit(solution)/shard_map/reduce_scatter | solution.py:54
  55.8 89.5 %copy-start.1 = (bf16[320,4096]{1,0:T(8,128)(2,1)S(1)}, bf16[320,4096]{1,0:T(8,128)(2,1)}, u32[]{:S(2)}) copy-start(bf16[320,4096]{1,0:T(8,128)(2,1)} %all-gather.5.cloned.1.call-done) | copy-start | bytes 7864324
  61.1 134.8 %all-gather.7.cloned.1.call-start = ((), (), s32[]{:S(2)}) async-start(), calls=%async_computation.6 | async-start | bytes 2228224 | tf_op jit(solution)/shard_map/all_gather | solution.py:64
  145.2 140.3 %reduce-scatter.13.cloned.1.call-start = ((), (), s32[]{:S(2)}) async-start(), calls=%async_computation.11 | async-start | bytes 6684672
  149.9 202.9 %reduce-scatter.9.cloned.1.call-start = ((), (), s32[]{:S(2)}) async-start(), calls=%async_computation.7 | async-start | bytes 5570560 | tf_op jit(solution)/shard_map/reduce_scatter | solution.py:68
  200.6 0.7 copy-start.10
  200.6 84.9 %copy-start.8 = (bf16[24,4096]{1,0:T(8,128)(2,1)S(1)}, bf16[24,4096]{1,0:T(8,128)(2,1)}, u32[]{:S(2)}) copy-start(bf16[24,4096]{1,0:T(8,128)(2,1)} %param.15) | copy-start | bytes 589828
  200.6 152.2 %copy-start.4 = (f32[320,256]{1,0:T(8,128)S(1)}, f32[320,256]{1,0:T(8,128)}, u32[]{:S(2)}) copy-start(f32[320,256]{1,0:T(8,128)} %param.18) | copy-start | bytes 983044
  200.6 205.6 %all-gather.11.cloned.1.call-start = ((), (), s32[]{:S(2)}) async-start(), calls=%async_computation.9 | async-start | bytes 3342336 | tf_op jit(solution)/shard_map/all_gather | solution.py:88
  287.3 164.4 %all-gather.9.cloned.1.call-start = ((), (), s32[]{:S(2)}) async-start(), calls=%async_computation.8 | async-start | bytes 5570560 | tf_op jit(solution)/shard_map/all_gather | solution.py:73
  354.8 224.7 %reduce-scatter.11.cloned.1.call-start = ((), (), s32[]{:S(2)}) async-start(), calls=%async_computation.10 | async-start | bytes 5570560 | tf_op jit(solution)/shard_map/reduce_scatter | solution.py:109
  514.3 65.2 %copy-start.3 = (f32[320,256]{1,0:T(8,128)S(1)}, f32[320,256]{1,0:T(8,128)}, u32[]{:S(2)}) copy-start(f32[320,256]{1,0:T(8,128)} %param.17) | copy-start | bytes 983044
  514.3 65.2 %copy-start.5 = (f32[320,256]{1,0:T(8,128)S(1)}, f32[320,256]{1,0:T(8,128)}, u32[]{:S(2)}) copy-start(f32[320,256]{1,0:T(8,128)} %param.21) | copy-start | bytes 983044
  514.3 65.2 %copy-start.6 = (f32[320,256]{1,0:T(8,128)S(1)}, f32[320,256]{1,0:T(8,128)}, u32[]{:S(2)}) copy-start(f32[320,256]{1,0:T(8,128)} %param.19) | copy-start | bytes 983044
  514.3 65.2 %copy-start.7 = (f32[320,256]{1,0:T(8,128)S(1)}, f32[320,256]{1,0:T(8,128)}, u32[]{:S(2)}) copy-start(f32[320,256]{1,0:T(8,128)} %param.20) | copy-start | bytes 983044
Sparse Core Ops, SparseCore 0:
  10.3 45.4 all-gather.4
  61.2 82.3 reduce-scatter.6
  146.6 49.2 all-gather.6
  199.4 86.0 reduce-scatter.12
  287.9 64.8 reduce-scatter.8
  355.7 50.5 all-gather.10
  408.7 42.9 all-gather.8
  514.5 64.9 reduce-scatter.10
where the time goes:
time: 589 us; the launch traced here: 588 us
  waiting for transfers between devices  487 us (83%)
  matrix products  36.8 us (6%)
  blocking collectives  34.3 us (6%)
  between operations  14.2 us (2%)
  other arithmetic  9.32 us (2%)
    unnamed x9, waiting for transfers between devices  84.3 us
    reduce_scatter x1, waiting for transfers between devices, on_device(): lax.psum_scatter(jnp.dot(block_x, w_half, preferred_element_type=jnp.floa...  82.5 us
    reduce_scatter x1, waiting for transfers between devices, on_device(): lax.psum_scatter(public_grad, 'replica', scatter_dimension=1, tiled=True)  65.5 us
    reduce_scatter x1, waiting for transfers between devices, on_device(): lax.psum_scatter(summed, 'replica', scatter_dimension=1, tiled=True)  65.1 us
    all_gather x1, waiting for transfers between devices, on_device(): private_delta = lax.all_gather(local_delta, 'tile', axis=0, tiled=True)  51.4 us
    all_gather x1, waiting for transfers between devices, on_device(): lax.all_gather(weight.astype(jnp.bfloat16), 'replica', axis=1, tiled=True)  46.8 us
    all_gather x1, waiting for transfers between devices, on_device(): lax.all_gather(public_delta, 'tile', axis=0, tiled=True)  45.9 us
    all_gather x1, waiting for transfers between devices, on_device(): precond = lax.all_gather(precond_owned, 'replica', axis=1, tiled=True)  45.5 us
  transfers between devices with their start and end apart: 8, of which 8 were waited for; matrix products, arithmetic and copies ran while one was open for 2% of the time, Pallas kernels for 0%

commit v1 on v0

--- a/solution.py
+++ b/solution.py
@@ -70,7 +70,10 @@
     ) / math.sqrt(public_total)
     new_public = beta_public * public_moment + (1.0 - beta_public) * grad_owned * grad_owned
     precond_owned = 1.0 / (jnp.sqrt(new_public) + public_epsilon)
-    precond = lax.all_gather(precond_owned, "replica", axis=1, tiled=True)
+    precond = jnp.concatenate(
+        lax.all_to_all(jnp.stack([precond_owned] * lax.axis_size("replica")), "replica", 0, 0),
+        axis=1,
+    )
     counts_row = token_counts[0]
     slots_all = private_tokens.shape[0]
     slot_rows = private_targets.shape[0]

time: 589 us -> 548 us (0.930)
  waiting for transfers between devices: 487 us -> 432 us
  local copies, waits for them, and re-layouts: 4.62 us -> 14.3 us
    all_gather x1 -> x0, waiting for transfers between devices: 45.5 us -> none  [on_device(): precond = lax.all_gather(precond_owned, 'replica', axis=1, tiled=True)]
    all_gather x1, waiting for transfers between devices: 51.4 us -> 11.3 us  [on_device(): private_delta = lax.all_gather(local_delta, 'tile', axis=0, tiled=True)]
    all_to_all x0 -> x1, waiting for transfers between devices: none -> 35.4 us  [on_device(): lax.all_to_all(jnp.stack([precond_owned] * lax.axis_size('replica')), 're...]
    reduce_scatter x1, waiting for transfers between devices: 65.5 us -> 58.8 us  [on_device(): lax.psum_scatter(public_grad, 'replica', scatter_dimension=1, tiled=True)]
    unnamed x9 -> x8, waiting for transfers between devices: 84.3 us -> 79.4 us
  transfers between devices with their start and end apart: 8 -> 8, of which waited for: 8 -> 8; matrix products, arithmetic and copies ran while one was open for 2% -> 3% of each run, Pallas kernels for 0% -> 0%
where the time goes in v1:
time: 548 us; the launch traced here: 547 us
  waiting for transfers between devices  432 us (79%)
  matrix products  36.6 us (7%)
  blocking collectives  33.3 us (6%)
  local copies, waits for them, and re-layouts  14.3 us (3%)
  between operations  14.2 us (3%)
  other arithmetic  9.21 us (2%)
    reduce_scatter x1, waiting for transfers between devices, on_device(): lax.psum_scatter(jnp.dot(block_x, w_half, preferred_element_type=jnp.floa...  82.5 us
    unnamed x8, waiting for transfers between devices  79.4 us
    reduce_scatter x1, waiting for transfers between devices, on_device(): lax.psum_scatter(summed, 'replica', scatter_dimension=1, tiled=True)  67.7 us
    reduce_scatter x1, waiting for transfers between devices, on_device(): lax.psum_scatter(public_grad, 'replica', scatter_dimension=1, tiled=True)  58.8 us
    all_gather x1, waiting for transfers between devices, on_device(): lax.all_gather(public_delta, 'tile', axis=0, tiled=True)  50.6 us
    all_gather x1, waiting for transfers between devices, on_device(): lax.all_gather(weight.astype(jnp.bfloat16), 'replica', axis=1, tiled=True)  46.8 us
    all_to_all x1, waiting for transfers between devices, on_device(): lax.all_to_all(jnp.stack([precond_owned] * lax.axis_size('replica')), 're...  35.4 us
    psum x1, blocking collectives, on_device(): squares = lax.psum(partial_norms, 'tile')  33.3 us
  transfers between devices with their start and end apart: 8, of which 8 were waited for; matrix products, arithmetic and copies ran while one was open for 3% of the time, Pallas kernels for 0%

profile of v1, /device:TPU:2, one launch (start us, length us, event | category | flops | bytes accessed | tf_op | source)
XLA Modules:
  0.0 547.0 jit_solution(4225169907690063380)
XLA Ops:
  7.2 0.0 copy-start
  7.2 0.0 all-gather.4.cloned.1.call-start
  7.2 1.7 convert_element_type.23
  8.9 0.0 all-gather.4.cloned.1.call-update
  8.9 0.0 copy-start.9
  9.0 0.0 reduce-scatter.7.cloned.1.call-start
  9.0 46.8 %all-gather.4.cloned.1.call-done = bf16[320,4096]{1,0:T(8,128)(2,1)} async-done(((bf16[320,256]{1,0:T(8,128)(2,1)}), bf16[320,4096]{1,0:T(8,128)(2,1)}) %all-gather.4.cloned.1.call-update) | async-done | bytes 2621456 | tf_op jit(solution)/shard_map/all_gather | solution.py:51
  55.8 0.0 copy-done
  55.8 5.1 fusion.11
  60.9 0.0 reduce-scatter.7.cloned.1.call-update
  60.9 0.0 all-gather.6.cloned.1.call-start
  60.9 82.5 %reduce-scatter.7.cloned.1.call-done = f32[16,4096]{1,0:T(8,128)} async-done(((f32[256,4096]{1,0:T(8,128)}), f32[16,4096]{1,0:T(8,128)}) %reduce-scatter.7.cloned.1.call-update) | async-done | bytes 262160 | tf_op jit(solution)/shard_map/reduce_scatter | solution.py:54
  143.4 0.0 copy-done.9
  143.4 1.6 subtract_convert_fusion
  145.0 0.0 all-gather.6.cloned.1.call-update
  145.1 0.0 reduce-scatter.9.cloned.1.call-start
  145.1 50.6 %all-gather.6.cloned.1.call-done = bf16[256,4096]{1,0:T(8,128)(2,1)} async-done(((bf16[16,4096]{1,0:T(8,128)(2,1)}), bf16[256,4096]{1,0:T(8,128)(2,1)}) %all-gather.6.cloned.1.call-update) | async-done | bytes 2097168 | tf_op jit(solution)/shard_map/all_gather | solution.py:64
  195.7 4.8 convolution_bitcast_fusion.1
  200.5 0.0 copy-start.1
  200.5 0.0 copy-start.2
  200.5 0.0 reduce-scatter.9.cloned.1.call-update
  200.5 0.0 reduce-scatter.13.cloned.1.call-start
  200.6 1.7 copy-done.1
  202.2 0.0 copy-done.2
  202.2 4.5 fusion.12
  206.7 0.0 copy-start.4
  206.7 0.0 reduce-scatter.13.cloned.1.call-update
  206.7 58.8 %reduce-scatter.9.cloned.1.call-done = f32[320,256]{1,0:T(8,128)} async-done(((f32[320,4096]{1,0:T(8,128)}), f32[320,256]{1,0:T(8,128)}) %reduce-scatter.9.cloned.1.call-update) | async-done | bytes 327696 | tf_op jit(solution)/shard_map/reduce_scatter | solution.py:68
  265.5 0.0 copy-done.4
  265.5 1.8 add_divide_fusion
  267.4 2.8 stack.2
  270.1 0.0 copy-start.10
  270.1 4.7 all-to-all-start
  274.9 0.0 all-gather.8.cloned.1.call-start
  274.9 0.0 copy-done.10
  274.9 0.1 select_reduce_fusion.1
  275.1 79.3 %reduce-scatter.13.cloned.1.call-done = f32[24,4096]{1,0:T(8,128)} async-done(((f32[384,4096]{1,0:T(8,128)}), f32[24,4096]{1,0:T(8,128)}) %reduce-scatter.13.cloned.1.call-update) | async-done | bytes 393232
  354.3 0.0 copy-done.8
  354.4 1.8 select_convert_fusion
  356.1 0.0 all-gather.8.cloned.1.call-update
  356.1 0.0 reduce-scatter.11.cloned.1.call-start
  356.2 35.4 %all-to-all-done = f32[16,320,256]{2,1,0:T(8,128)} async-done(((f32[16,320,256]{2,1,0:T(8,128)}), f32[16,320,256]{2,1,0:T(8,128)}, u32[]{:S(2)}, u32[]{:S(2)}) %all-to-all-start) | async-done | bytes 5242912 | tf_op jit(solution)/shard_map/all_to_all | solution.py:74
  391.6 5.8 %copy.16 = f32[16,40,8,256]{3,2,0,1:T(8,128)} copy(f32[16,40,8,256]{3,2,1,0:T(8,128)} %bitcast.7) | data formatting | bytes 10485760 | tf_op jit(solution)/shard_map/reshape | solution.py:73
  397.4 11.3 %all-gather.8.cloned.1.call-done = bf16[384,4096]{1,0:T(8,128)(2,1)} async-done(((bf16[24,4096]{1,0:T(8,128)(2,1)}), bf16[384,4096]{1,0:T(8,128)(2,1)}) %all-gather.8.cloned.1.call-update) | async-done | bytes 3145744 | tf_op jit(solution)/shard_map/all_gather | solution.py:91
  408.7 20.8 %while.10 = (s32[]{:T(128)}, f32[3]{0:T(128)S(1)}, s32[3]{0:T(128)S(1)}, bf16[384,320]{0,1:T(8,128)(2,1)S(1)}, bf16[384,4096]{1,0:T(8,128)(2,1)}, /*index=5*/f32...) while((s32[]{:T(128)}, f32[3]{0:T(128)S(1)}, s32[3]{0:T(128)S(1)}, ...), condition=%wide.region_6.7_spmd, body=%wide.region_4.6_spmd.sunk | while | flops 339476480 | bytes 6374575 | solution.py:102
  408.7 0.6 dynamic_slice.19
  410.0 4.9 fusion.25
  414.9 0.8 dynamic_update_slice.5
  415.7 0.6 dynamic_slice.19
  416.9 5.0 fusion.25
  421.9 0.8 dynamic_update_slice.5
  422.6 0.6 dynamic_slice.19
  423.9 5.0 fusion.25
  428.8 0.8 dynamic_update_slice.5
  429.6 33.3 %psum.7 = f32[3]{0:T(128)S(1)} all-reduce(f32[3]{0:T(128)S(1)} %get-tuple-element.36), channel_id=1, replica_groups=mesh['replica'=16,'tile'=16] {'tile'}, use_global_device_ids=true, to_apply=%region_7.8 | all-reduce | flops 3 | bytes 24 | tf_op jit(solution)/shard_map/psum | solution.py:103
  462.9 0.1 select_reduce_fusion
  462.9 7.4 %fusion.5 = f32[320,4096]{1,0:T(8,128)} fusion(f32[320,4096]{1,0:T(8,128)} %get-tuple-element.128, bf16[384,320]{0,1:T(8,128)(2,1)S(1)} %get-tuple-element.142, bf16[384,4096]{1,0:T(8,128)(2,1)} %get-tuple-element.136, f32[384]{0:T(512)S(1)} %select_reduce_fusion), kind=kOutput, calls=%fused_computation.9 | convolution fusion | flops 1012662272 | bytes 13878784 | tf_op jit(solution)/shard_map/dot_general | solution.py:109
  470.4 0.0 reduce-scatter.11.cloned.1.call-update
  470.4 67.7 %reduce-scatter.11.cloned.1.call-done = f32[320,256]{1,0:T(8,128)} async-done(((f32[320,4096]{1,0:T(8,128)}), f32[320,256]{1,0:T(8,128)}) %reduce-scatter.11.cloned.1.call-update) | async-done | bytes 327696 | tf_op jit(solution)/shard_map/reduce_scatter | solution.py:112
  538.1 0.0 copy-done.3
  538.1 0.0 copy-done.5
  538.1 0.0 copy-done.6
  538.1 0.0 copy-done.7
  538.1 2.1 divide_subtract_fusion
  (11 shorter events, 0.1 us)
Async XLA Ops:
  7.2 48.6 %copy-start = (bf16[256,320]{0,1:T(8,128)(2,1)S(1)}, bf16[256,320]{0,1:T(8,128)(2,1)}, u32[]{:S(2)}) copy-start(bf16[256,320]{0,1:T(8,128)(2,1)} %param.12) | copy-start | bytes 491524
  7.2 48.6 %all-gather.4.cloned.1.call-start = ((), (), s32[]{:S(2)}) async-start(), calls=%async_computation.5 | async-start | bytes 2785280 | tf_op jit(solution)/shard_map/all_gather | solution.py:51
  8.9 134.5 %copy-start.9 = (bf16[16,4096]{1,0:T(8,128)(2,1)S(1)}, bf16[16,4096]{1,0:T(8,128)(2,1)}, u32[]{:S(2)}) copy-start(bf16[16,4096]{1,0:T(8,128)(2,1)} %param.13) | copy-start | bytes 393220
  9.0 134.5 %reduce-scatter.7.cloned.1.call-start = ((), (), s32[]{:S(2)}) async-start(), calls=%async_computation.6 | async-start | bytes 4456448 | tf_op jit(solution)/shard_map/reduce_scatter | solution.py:54
  60.9 134.8 %all-gather.6.cloned.1.call-start = ((), (), s32[]{:S(2)}) async-start(), calls=%async_computation.7 | async-start | bytes 2228224 | tf_op jit(solution)/shard_map/all_gather | solution.py:64
  145.1 120.4 %reduce-scatter.9.cloned.1.call-start = ((), (), s32[]{:S(2)}) async-start(), calls=%async_computation.8 | async-start | bytes 5570560 | tf_op jit(solution)/shard_map/reduce_scatter | solution.py:68
  200.5 1.7 copy-start.1
  200.5 1.7 copy-start.2
  200.5 153.8 %reduce-scatter.13.cloned.1.call-start = ((), (), s32[]{:S(2)}) async-start(), calls=%async_computation.11 | async-start | bytes 6684672
  206.7 58.8 %copy-start.4 = (f32[320,256]{1,0:T(8,128)S(1)}, f32[320,256]{1,0:T(8,128)}, u32[]{:S(2)}) copy-start(f32[320,256]{1,0:T(8,128)} %param.18) | copy-start | bytes 983044
  270.1 4.8 copy-start.10
  270.1 84.2 %copy-start.8 = (bf16[24,4096]{1,0:T(8,128)(2,1)S(1)}, bf16[24,4096]{1,0:T(8,128)(2,1)}, u32[]{:S(2)}) copy-start(bf16[24,4096]{1,0:T(8,128)(2,1)} %param.15) | copy-start | bytes 589828
  270.1 121.5 %all-to-all-start = ((f32[16,320,256]{2,1,0:T(8,128)}), f32[16,320,256]{2,1,0:T(8,128)}, u32[]{:S(2)}, u32[]{:S(2)}) async-start(f32[16,320,256]{2,1,0:T(8,128)} %stack.2), calls=%async_computation.2 | async-start | bytes 10485760 | tf_op jit(solution)/shard_map/all_to_all | solution.py:74
  274.9 133.9 %all-gather.8.cloned.1.call-start = ((), (), s32[]{:S(2)}) async-start(), calls=%async_computation.9 | async-start | bytes 3342336 | tf_op jit(solution)/shard_map/all_gather | solution.py:91
  356.1 181.9 %reduce-scatter.11.cloned.1.call-start = ((), (), s32[]{:S(2)}) async-start(), calls=%async_computation.10 | async-start | bytes 5570560 | tf_op jit(solution)/shard_map/reduce_scatter | solution.py:112
  470.3 67.7 %copy-start.3 = (f32[320,256]{1,0:T(8,128)S(1)}, f32[320,256]{1,0:T(8,128)}, u32[]{:S(2)}) copy-start(f32[320,256]{1,0:T(8,128)} %param.17) | copy-start | bytes 983044
  470.4 67.7 %copy-start.5 = (f32[320,256]{1,0:T(8,128)S(1)}, f32[320,256]{1,0:T(8,128)}, u32[]{:S(2)}) copy-start(f32[320,256]{1,0:T(8,128)} %param.21) | copy-start | bytes 983044
  470.4 67.7 %copy-start.6 = (f32[320,256]{1,0:T(8,128)S(1)}, f32[320,256]{1,0:T(8,128)}, u32[]{:S(2)}) copy-start(f32[320,256]{1,0:T(8,128)} %param.19) | copy-start | bytes 983044
  470.4 67.7 %copy-start.7 = (f32[320,256]{1,0:T(8,128)S(1)}, f32[320,256]{1,0:T(8,128)}, u32[]{:S(2)}) copy-start(f32[320,256]{1,0:T(8,128)} %param.20) | copy-start | bytes 983044
Sparse Core Ops, SparseCore 0:
  10.3 45.4 all-gather.3
  61.0 82.3 reduce-scatter.6
  146.4 49.2 all-gather.5
  200.6 64.8 reduce-scatter.8
  269.1 85.2 reduce-scatter.12
  357.3 51.4 all-gather.7
  470.5 67.5 reduce-scatter.10
